TPU v7x, 128 devices: a whole 4x4x4 slice. The times are simulated.
128 devices in a mesh: req: 16 (over x, z), head: 8 (over y, core).
Axes of the slice: x: 4, y: 4, z: 4, core: 2. Of those that a mesh axis runs over, the one named last changes fastest.
Arguments:
- hidden: bfloat16 [512, 2048], P('req', 'head'), may hold values from -6 to 6
- lengths: int32 [512], P('req'), may hold values from 1 to 384, as said below
- expert_ids: int32 [512, 8], P('req'), may hold values from 0 to 63, all different within a row
- route_weights: float32 [512, 8], P('req'), may hold values from 0.25 to 2.5
- w_qkv: bfloat16 [3, 2048, 2048], P(None, None, 'head'), may hold values from -0.125 to 0.125
- w_out: bfloat16 [2048, 2048], P('head'), may hold values from -0.125 to 0.125
- k_cache: bfloat16 [512, 384, 16, 128], P('req', None, 'head'), may hold values from -400 to 400
- v_cache: bfloat16 [512, 384, 16, 128], P('req', None, 'head'), may hold values from -12 to 12
- w_in: bfloat16 [2048, 64, 2048], P(None, 'head', 'req'), may hold values from -0.125 to 0.125
- w_down: bfloat16 [64, 1024, 2048], P('head', 'req'), may hold values from -0.1875 to 0.1875
Outputs:
- output: bfloat16 [512, 2048], P('req', 'head')
Inputs may be any that keep to these rules, and one draw needn't show every extreme that they name: `lengths`: some request has exactly 384 cached positions.
All inputs are finite; a program needn't handle non-finite values.
Results may differ from a plain program's by a relative error of at most 0.023.
Values may be sent and summed in bfloat16 or wider, within the bound.
A program may use at most 128 MiB of HBM per device.

v0:
```python
import jax
import jax.numpy as jnp
from jax import lax
from jax.sharding import PartitionSpec as P

UNIT_BLOCK = 64
KEY_BLOCK = 128
rope_theta = 50000.0
norm_eps = 1e-05


def over_all(shard, axis, dim, work):
    return work(lax.all_gather(shard, axis, axis=dim, tiled=True), jnp.int32(0))


def rotate(values, positions):
    half_dim = values.shape[-1] // 2
    freqs = rope_theta ** (-jnp.arange(half_dim, dtype=jnp.float32) / half_dim)
    angles = positions.astype(jnp.float32)[:, None] * freqs[None, :]
    cosine = jnp.cos(angles)[:, None, :]
    sine = jnp.sin(angles)[:, None, :]
    first_half = values[..., :half_dim]
    second_half = values[..., half_dim:]
    return jnp.concatenate(
        [first_half * cosine - second_half * sine, second_half * cosine + first_half * sine],
        axis=-1,
    )


def rms_normed(values):
    return (
        values * lax.rsqrt(jnp.mean(values * values, axis=-1, keepdims=True) + norm_eps)
    ).astype(jnp.bfloat16)


def per_device(
    hidden, lengths, expert_ids, route_weights, w_qkv, w_out, k_cache, v_cache, w_in, w_down
):
    full_rows = lax.all_gather(hidden, "head", axis=1, tiled=True)
    hidden_f = full_rows.astype(jnp.float32)
    normed = rms_normed(hidden_f)
    req_local = hidden.shape[0]
    col_width = hidden.shape[1]
    heads_local = k_cache.shape[2]
    head_size = k_cache.shape[3]
    cache_len = k_cache.shape[1]
    projected = jnp.einsum("td,cdn->ctn", normed, w_qkv, preferred_element_type=jnp.float32)
    projected = projected.reshape(3, req_local, heads_local, head_size)
    query = rotate(projected[0], lengths).astype(jnp.bfloat16)
    key_new = rotate(projected[1], lengths).astype(jnp.bfloat16)
    value_new = projected[2].astype(jnp.bfloat16)
    score_scale = head_size ** (-0.5)
    block_count = (jnp.max(lengths) + KEY_BLOCK - 1) // KEY_BLOCK

    def score_block(block_idx, buffer):
        keys_block = lax.dynamic_slice_in_dim(k_cache, block_idx * KEY_BLOCK, KEY_BLOCK, 1)
        block_scores = (
            jnp.einsum("rhd,rlhd->rhl", query, keys_block, preferred_element_type=jnp.float32)
            * score_scale
        )
        return lax.dynamic_update_slice_in_dim(buffer, block_scores, block_idx * KEY_BLOCK, 2)

    buffer = jnp.full((req_local, heads_local, cache_len), -jnp.inf, jnp.float32)
    buffer = lax.fori_loop(0, block_count, score_block, buffer)
    positions = jnp.arange(cache_len, dtype=jnp.int32)
    scores = jnp.where(positions[None, None, :] < lengths[:, None, None], buffer, -jnp.inf)
    self_score = (
        jnp.einsum("rhd,rhd->rh", query, key_new, preferred_element_type=jnp.float32) * score_scale
    )
    row_top = jnp.maximum(jnp.max(scores, axis=-1), self_score)
    exponent = jnp.exp(scores - row_top[:, :, None])
    self_exp = jnp.exp(self_score - row_top)
    denominator = jnp.sum(exponent, axis=-1) + self_exp
    weights = (exponent / denominator[:, :, None]).astype(jnp.bfloat16)
    self_weight = (self_exp / denominator).astype(jnp.bfloat16)

    def value_block(block_idx, accum):
        weights_block = lax.dynamic_slice_in_dim(weights, block_idx * KEY_BLOCK, KEY_BLOCK, 2)
        values_block = lax.dynamic_slice_in_dim(v_cache, block_idx * KEY_BLOCK, KEY_BLOCK, 1)
        return accum + jnp.einsum(
            "rhl,rlhd->rhd", weights_block, values_block, preferred_element_type=jnp.float32
        )

    accum = lax.fori_loop(
        0, block_count, value_block, jnp.zeros((req_local, heads_local, head_size), jnp.float32)
    )
    accum = accum + self_weight.astype(jnp.float32)[:, :, None] * value_new.astype(jnp.float32)
    attended = accum.astype(jnp.bfloat16).reshape(req_local, heads_local * head_size)
    head_terms = jnp.dot(attended, w_out, preferred_element_type=jnp.float32)
    resid = hidden_f + lax.psum(head_terms.astype(jnp.bfloat16), "head").astype(jnp.float32)
    mixed = rms_normed(resid)
    experts_local = w_down.shape[0]
    units_local = w_down.shape[1]
    width = w_in.shape[0]
    expert_base = lax.axis_index("head") * experts_local + jnp.arange(
        experts_local, dtype=jnp.int32
    )
    w_in_flat = w_in.reshape(width, experts_local * 2 * units_local)
    w_down_flat = w_down.reshape(experts_local * units_local, width)

    def expert_hidden(pieces):
        token_rows, token_ids, token_weights = pieces
        row_count = token_rows.shape[0]
        matches = (token_ids[:, :, None] == expert_base[None, None, :]).astype(jnp.float32)
        combined = jnp.sum(token_weights[:, :, None] * matches, axis=1)
        gate_up = jnp.dot(token_rows, w_in_flat, preferred_element_type=jnp.float32)
        gate_up = gate_up.reshape(
            row_count, experts_local, units_local // UNIT_BLOCK, 2, UNIT_BLOCK
        )
        gate = gate_up[:, :, :, 0, :]
        upward = gate_up[:, :, :, 1, :]
        units = (combined[:, :, None, None] * (jax.nn.silu(gate) * upward)).astype(jnp.bfloat16)
        return units.reshape(row_count, experts_local * units_local)

    gathered = over_all(
        (mixed, expert_ids, route_weights.astype(jnp.bfloat16)),
        "req",
        0,
        lambda piece, start: expert_hidden((piece[0], piece[1], piece[2].astype(jnp.float32))),
    )
    token_sums = lax.psum_scatter(
        jnp.dot(gathered, w_down_flat, preferred_element_type=jnp.float32).astype(jnp.bfloat16),
        "req",
        scatter_dimension=0,
        tiled=True,
    )
    moe_share = lax.psum_scatter(token_sums, "head", scatter_dimension=1, tiled=True).astype(
        jnp.float32
    )
    resid_share = lax.dynamic_slice_in_dim(resid, lax.axis_index("head") * col_width, col_width, 1)
    return (resid_share + moe_share).astype(jnp.bfloat16)


def solution(mesh):
    in_specs = (
        P("req", "head"),
        P("req"),
        P("req", None),
        P("req", None),
        P(None, None, "head"),
        P("head", None),
        P("req", None, "head", None),
        P("req", None, "head", None),
        P(None, "head", "req"),
        P("head", "req", None),
    )
    out_specs = P("req", "head")
    return jax.shard_map(
        per_device, mesh=mesh, in_specs=in_specs, out_specs=out_specs, check_vma=False
    )
```

profile of v0, /device:TPU:0, one launch (start us, length us, event | category | flops | bytes accessed | tf_op | source)
XLA Modules:
  0.0 295.3 jit_solution(10941780529254591769)
XLA Ops:
  6.5 1.5 fusion.28
  8.8 0.7 iota_compare_fusion
  9.5 13.6 %all_gather.12 = bf16[32,2048]{1,0:T(8,128)(2,1)S(1)} all-gather(bf16[32,256]{1,0:T(8,128)(2,1)} %param.14), channel_id=1, replica_groups=mesh['req'=16,'head'=8] {'head'}, dimensions={1}, use_global_device_ids=true | all-gather | bytes 147456 | tf_op jit(solution)/shard_map/all_gather | solution.py:39
  23.1 0.1 fusion.14
  23.3 0.7 convolution_bitcast_fusion
  24.1 0.1 multiply_cosine_fusion
  24.2 0.2 subtract_convert_fusion.1
  24.4 0.2 fusion.20
  24.6 13.6 %while.20 = (s32[]{:T(128)}, f32[32,2,384]{2,1,0:T(2,128)S(1)}, s32[]{:T(128)}, bf16[32,384,2,128]{3,2,1,0:T(2,128)(2,1)}, bf16[32,2,128]{2,1,0:T(2,128)(2,1)S(1...) while((s32[]{:T(128)}, f32[32,2,384]{2,1,0:T(2,128)S(1)}, s32[]{:T(128)}, ...), condition=%wide.region_3.4_spmd, body=%wide.region_2.3_spmd.sunk | while | flops 2105350 | bytes 6406299 | solution.py:64
  24.6 3.3 %constant_dynamic-slice_fusion.4 = bf16[32,128,2,128]{3,2,1,0:T(2,128)(2,1)S(1)} fusion(bf16[32,384,2,128]{3,2,1,0:T(2,128)(2,1)} %get-tuple-element.186, s32[]{:T(128)S(6)} %select_n.34), kind=kLoop, calls=%fused_computation.4.clone.1 | loop fusion | bytes 4194308 | tf_op jit(solution)/shard_map/while/body/dynamic_slice | solution.py:56
  27.9 1.2 fusion.42
  29.1 0.1 multiply_dynamic-update-slice_fusion.2
  29.2 3.3 %constant_dynamic-slice_fusion.4 = bf16[32,128,2,128]{3,2,1,0:T(2,128)(2,1)S(1)} fusion(bf16[32,384,2,128]{3,2,1,0:T(2,128)(2,1)} %get-tuple-element.186, s32[]{:T(128)S(6)} %select_n.34), kind=kLoop, calls=%fused_computation.4.clone.1 | loop fusion | bytes 4194308 | tf_op jit(solution)/shard_map/while/body/dynamic_slice | solution.py:56
  32.5 1.2 fusion.42
  33.6 0.1 multiply_dynamic-update-slice_fusion.2
  33.7 3.3 %constant_dynamic-slice_fusion.4 = bf16[32,128,2,128]{3,2,1,0:T(2,128)(2,1)S(1)} fusion(bf16[32,384,2,128]{3,2,1,0:T(2,128)(2,1)} %get-tuple-element.186, s32[]{:T(128)S(6)} %select_n.34), kind=kLoop, calls=%fused_computation.4.clone.1 | loop fusion | bytes 4194308 | tf_op jit(solution)/shard_map/while/body/dynamic_slice | solution.py:56
  37.0 1.2 fusion.42
  38.2 0.1 multiply_dynamic-update-slice_fusion.2
  38.2 0.1 fusion.19
  38.4 0.2 fusion.24
  38.6 0.2 divide_convert_fusion
  38.9 12.1 %while.21 = (s32[]{:T(128)}, f32[32,2,128]{2,1,0:T(2,128)S(1)}, s32[]{:T(128)}, bf16[32,2,384]{2,1,0:T(2,128)(2,1)S(1)}, bf16[32,384,2,128]{3,2,1,0:T(2,128)(2,1...) while((s32[]{:T(128)}, f32[32,2,128]{2,1,0:T(2,128)S(1)}, s32[]{:T(128)}, ...), condition=%wide.region_7.8_spmd, body=%wide.region_6.7_spmd.sunk | while | flops 2105350 | bytes 6471835 | solution.py:84
  38.9 3.3 %constant_dynamic-slice_fusion.5 = bf16[32,128,2,128]{3,2,1,0:T(2,128)(2,1)S(1)} fusion(bf16[32,384,2,128]{3,2,1,0:T(2,128)(2,1)} %get-tuple-element.214, s32[]{:T(128)S(6)} %select_n.35), kind=kLoop, calls=%fused_computation.9.clone.1 | loop fusion | bytes 4194308 | tf_op jit(solution)/shard_map/while/body/dynamic_slice | solution.py:79
  42.2 0.6 fusion.45
  42.9 3.3 %constant_dynamic-slice_fusion.5 = bf16[32,128,2,128]{3,2,1,0:T(2,128)(2,1)S(1)} fusion(bf16[32,384,2,128]{3,2,1,0:T(2,128)(2,1)} %get-tuple-element.214, s32[]{:T(128)S(6)} %select_n.35), kind=kLoop, calls=%fused_computation.9.clone.1 | loop fusion | bytes 4194308 | tf_op jit(solution)/shard_map/while/body/dynamic_slice | solution.py:79
  46.2 0.6 fusion.45
  46.9 3.3 %constant_dynamic-slice_fusion.5 = bf16[32,128,2,128]{3,2,1,0:T(2,128)(2,1)S(1)} fusion(bf16[32,384,2,128]{3,2,1,0:T(2,128)(2,1)} %get-tuple-element.214, s32[]{:T(128)S(6)} %select_n.35), kind=kLoop, calls=%fused_computation.9.clone.1 | loop fusion | bytes 4194308 | tf_op jit(solution)/shard_map/while/body/dynamic_slice | solution.py:79
  50.2 0.7 fusion.45
  51.0 0.1 add_convert_fusion.1
  51.1 2.2 convolution_convert_fusion.1
  53.3 60.9 %all-reduce.2.cloned.1.call-done = bf16[32,2048]{1,0:T(8,128)(2,1)} async-done(((bf16[32,2048]{1,0:T(8,128)(2,1)}), bf16[32,2048]{1,0:T(8,128)(2,1)}) %all-reduce.2.cloned.1.call-update) | async-done | bytes 131088 | tf_op jit(solution)/shard_map/psum | solution.py:90
  114.3 1.1 convert_add_fusion
  115.3 1.6 multiply_convert_fusion
  117.0 5.3 %copy.57 = bf16[256,8,8,128]{3,1,2,0:T(8,128)(2,1)} copy(bf16[256,8,8,128]{3,2,1,0:T(8,128)(2,1)} %bitcast.70) | data formatting | bytes 8388608
  122.3 6.5 %copy.27 = bf16[1024,2048]{1,0:T(8,128)(2,1)} copy(bf16[1024,2048]{0,1:T(8,128)(2,1)} %bitcast.69) | data formatting | bytes 8388608 | tf_op jit(solution)/shard_map/dot_general | solution.py:106
  128.8 23.5 %all-gather.1 = bf16[16,32,8]{1,2,0:T(8,128)(2,1)S(1)} all-gather(bf16[1,32,8]{1,2,0:T(8,128)(2,1)S(1)} %convert_bitcast_fusion), channel_id=1, replica_groups=mesh['req'=16,'head'=8] {'req'}, dimensions={0}, use_global_device_ids=true | all-gather | bytes 8704 | tf_op jit(solution)/shard_map/all_gather | solution.py:13
  152.3 0.1 reshape.224
  152.4 23.1 %all-gather = s32[16,32,8]{1,2,0:T(8,128)S(1)} all-gather(s32[1,32,8]{1,2,0:T(8,128)} %bitcast.77), channel_id=1, replica_groups=mesh['req'=16,'head'=8] {'req'}, dimensions={0}, use_global_device_ids=true | all-gather | bytes 17408 | tf_op jit(solution)/shard_map/all_gather | solution.py:13
  175.6 0.1 reshape.221
  175.7 0.1 select_reduce_fusion
  175.8 5.2 %fusion.8 = f32[512,8,1,2,64]{0,4,3,1,2:T(8,128)S(1)} fusion(bf16[8,2,64,2048]{3,2,1,0:T(8,128)(2,1)} %bitcast.71, bf16[512,2048]{1,0:T(8,128)(2,1)} %all-gather.4.cloned.1.call-done), kind=kOutput, calls=%fused_computation.15 | convolution fusion | flops 2147483648 | bytes 8388608 | tf_op jit(solution)/shard_map/dot_general | solution.py:106
  181.0 0.3 fusion.13
  181.3 1.2 copy-done.2
  182.6 2.6 convolution_convert_fusion
  185.2 0.0 reduce-scatter.5.cloned.1.call-start
  185.3 70.5 %reduce-scatter.3.cloned.1.call-done = bf16[32,2048]{1,0:T(8,128)(2,1)} async-done(((bf16[512,2048]{1,0:T(8,128)(2,1)}), bf16[32,2048]{1,0:T(8,128)(2,1)}) %reduce-scatter.3.cloned.1.call-update) | async-done | bytes 131088 | tf_op jit(solution)/shard_map/reduce_scatter | solution.py:121
  255.8 31.7 %reduce-scatter.5.cloned.1.call-done = bf16[32,256]{1,0:T(8,128)(2,1)} async-done(((bf16[32,2048]{1,0:T(8,128)(2,1)}), bf16[32,256]{1,0:T(8,128)(2,1)}) %reduce-scatter.5.cloned.1.call-update) | async-done | bytes 16400 | tf_op jit(solution)/shard_map/reduce_scatter | solution.py:127
  287.5 1.3 add_convert_fusion
  (35 shorter events, 0.5 us)
Async XLA Ops:
  6.5 16.7 %copy-start = (bf16[3,2048,256]{2,1,0:T(8,128)(2,1)S(1)}, bf16[3,2048,256]{2,1,0:T(8,128)(2,1)}, u32[]{:S(2)}) copy-start(bf16[3,2048,256]{2,1,0:T(8,128)(2,1)} %param.18) | copy-start | bytes 9437188
  6.5 107.7 %all-reduce.2.cloned.1.call-start = ((), (), s32[]{:S(2)}) async-start(), calls=%async_computation.2 | async-start | bytes 262144 | tf_op jit(solution)/shard_map/psum | solution.py:90
  53.3 122.5 %all-gather.4.cloned.1.call-start = ((), (), s32[]{:S(2)}) async-start(), calls=%async_computation.3 | async-start | bytes 2228224 | tf_op jit(solution)/shard_map/all_gather | solution.py:13
  117.0 138.8 %reduce-scatter.3.cloned.1.call-start = ((), (), s32[]{:S(2)}) async-start(), calls=%async_computation.4 | async-start | bytes 2228224 | tf_op jit(solution)/shard_map/reduce_scatter | solution.py:121
  122.3 6.5 %copy-start.1 = (f32[32,8]{0,1:T(8,128)S(1)}, f32[32,8]{0,1:T(8,128)}, u32[]{:S(2)}) copy-start(f32[32,8]{0,1:T(8,128)} %param.17) | copy-start | bytes 3076
  181.0 1.6 copy-start.2
  185.2 102.3 %reduce-scatter.5.cloned.1.call-start = ((), (), s32[]{:S(2)}) async-start(), calls=%async_computation.5 | async-start | bytes 147456 | tf_op jit(solution)/shard_map/reduce_scatter | solution.py:127
Sparse Core Ops, SparseCore 0:
  53.4 60.8 all-reduce.1
  117.1 44.3 all-gather.3
  185.4 70.3 reduce-scatter.2
  258.0 29.4 reduce-scatter.4
where the time goes:
time: 296 us; the launch traced here: 295 us
  waiting for transfers between devices  163 us (55%)
  blocking collectives  60.2 us (20%)
  local copies, waits for them, and re-layouts  33.1 us (11%)
  matrix products  16.1 us (5%)
  between operations  14 us (5%)
  other arithmetic  8.33 us (3%)
    reduce_scatter x1, waiting for transfers between devices, per_device(): lax.psum_scatter(jnp.dot(gathered, w_down_flat, preferred_element_type=jn...  70.5 us
    psum x1, waiting for transfers between devices, per_device(): lax.psum(head_terms.astype(jnp.bfloat16), 'head').astype(jnp.float32)  60.9 us
    all_gather x2, blocking collectives, over_all(): return work(lax.all_gather(shard, axis, axis=dim, tiled=True), jnp.int32(0))  46.6 us
    reduce_scatter x1, waiting for transfers between devices, per_device(): lax.psum_scatter(token_sums, 'head', scatter_dimension=1, tiled=True)  31.7 us
    all_gather x1, blocking collectives, per_device(): full_rows = lax.all_gather(hidden, 'head', axis=1, tiled=True)  13.6 us
    dynamic_slice x3, local copies, waits for them, and re-layouts, score_block(): lax.dynamic_slice_in_dim(k_cache, block_idx * KEY_BLOCK, KEY_BLOCK, 1)  9.85 us
    dynamic_slice x3, local copies, waits for them, and re-layouts, value_block(): lax.dynamic_slice_in_dim(v_cache, block_idx * KEY_BLOCK, KEY_BLOCK, 1)  9.85 us
    unnamed x8, local copies, waits for them, and re-layouts  6.58 us
  transfers between devices with their start and end apart: 4, of which 3 were waited for; matrix products, arithmetic and copies ran while one was open for 4% of the time, Pallas kernels for 0%

commit v1 on v0

--- a/solution.py
+++ b/solution.py
@@ -7,6 +7,11 @@
 KEY_BLOCK = 128
 rope_theta = 50000.0
 norm_eps = 1e-05
+
+
+def summed_here(x, axis):
+    pieces = lax.all_gather(x, axis)
+    return jnp.sum(pieces, axis=0)
 
 
 def over_all(shard, axis, dim, work):
@@ -87,7 +92,7 @@
     accum = accum + self_weight.astype(jnp.float32)[:, :, None] * value_new.astype(jnp.float32)
     attended = accum.astype(jnp.bfloat16).reshape(req_local, heads_local * head_size)
     head_terms = jnp.dot(attended, w_out, preferred_element_type=jnp.float32)
-    resid = hidden_f + lax.psum(head_terms.astype(jnp.bfloat16), "head").astype(jnp.float32)
+    resid = hidden_f + summed_here(head_terms.astype(jnp.bfloat16), "head").astype(jnp.float32)
     mixed = rms_normed(resid)
     experts_local = w_down.shape[0]
     units_local = w_down.shape[1]

time: 296 us -> 262 us (0.89)
  waiting for transfers between devices: 163 us -> 128 us
    psum x1 -> x0, waiting for transfers between devices: 60.9 us -> none  [per_device(): lax.psum(head_terms.astype(jnp.bfloat16), 'head').astype(jnp.float32)]
    all_gather x0 -> x1, waiting for transfers between devices: none -> 25 us  [summed_here(): pieces = lax.all_gather(x, axis)]
    unnamed x8 -> x10, local copies, waits for them, and re-layouts: 6.58 us -> 6.59 us
  transfers between devices with their start and end apart: 4 -> 4, of which waited for: 3 -> 3; matrix products, arithmetic and copies ran while one was open for 4% -> 5% of each run, Pallas kernels for 0% -> 0%
where the time goes in v1:
time: 262 us; the launch traced here: 261 us
  waiting for transfers between devices  128 us (49%)
  blocking collectives  60.2 us (23%)
  local copies, waits for them, and re-layouts  33.1 us (13%)
  matrix products  16.1 us (6%)
  between operations  14.1 us (5%)
  other arithmetic  8.68 us (3%)
    reduce_scatter x1, waiting for transfers between devices, per_device(): lax.psum_scatter(jnp.dot(gathered, w_down_flat, preferred_element_type=jn...  71.5 us
    all_gather x2, blocking collectives, over_all(): return work(lax.all_gather(shard, axis, axis=dim, tiled=True), jnp.int32(0))  46.6 us
    reduce_scatter x1, waiting for transfers between devices, per_device(): lax.psum_scatter(token_sums, 'head', scatter_dimension=1, tiled=True)  31.8 us
    all_gather x1, waiting for transfers between devices, summed_here(): pieces = lax.all_gather(x, axis)  25 us
    all_gather x1, blocking collectives, per_device(): full_rows = lax.all_gather(hidden, 'head', axis=1, tiled=True)  13.6 us
    dynamic_slice x3, local copies, waits for them, and re-layouts, score_block(): lax.dynamic_slice_in_dim(k_cache, block_idx * KEY_BLOCK, KEY_BLOCK, 1)  9.85 us
    dynamic_slice x3, local copies, waits for them, and re-layouts, value_block(): lax.dynamic_slice_in_dim(v_cache, block_idx * KEY_BLOCK, KEY_BLOCK, 1)  9.85 us
    unnamed x10, local copies, waits for them, and re-layouts  6.59 us
  transfers between devices with their start and end apart: 4, of which 3 were waited for; matrix products, arithmetic and copies ran while one was open for 5% of the time, Pallas kernels for 0%

profile of v1, /device:TPU:0, one launch (start us, length us, event | category | flops | bytes accessed | tf_op | source)
XLA Modules:
  0.0 260.9 jit_solution(17952878895754750406)
XLA Ops:
  6.5 1.5 fusion.28
  8.8 0.7 iota_compare_fusion
  9.5 13.6 %all_gather.18 = bf16[32,2048]{1,0:T(8,128)(2,1)S(1)} all-gather(bf16[32,256]{1,0:T(8,128)(2,1)} %param.14), channel_id=1, replica_groups=mesh['req'=16,'head'=8] {'head'}, dimensions={1}, use_global_device_ids=true | all-gather | bytes 147456 | tf_op jit(solution)/shard_map/all_gather | solution.py:44
  23.1 0.1 fusion.14
  23.3 0.7 convolution_bitcast_fusion
  24.1 0.1 multiply_cosine_fusion
  24.2 0.2 subtract_convert_fusion.1
  24.4 0.2 fusion.20
  24.6 13.6 %while.20 = (s32[]{:T(128)}, f32[32,2,384]{2,1,0:T(2,128)S(1)}, s32[]{:T(128)}, bf16[32,384,2,128]{3,2,1,0:T(2,128)(2,1)}, bf16[32,2,128]{2,1,0:T(2,128)(2,1)S(1...) while((s32[]{:T(128)}, f32[32,2,384]{2,1,0:T(2,128)S(1)}, s32[]{:T(128)}, ...), condition=%wide.region_3.4_spmd, body=%wide.region_2.3_spmd.sunk | while | flops 2105350 | bytes 6406299 | solution.py:69
  24.6 3.3 %constant_dynamic-slice_fusion.4 = bf16[32,128,2,128]{3,2,1,0:T(2,128)(2,1)S(1)} fusion(bf16[32,384,2,128]{3,2,1,0:T(2,128)(2,1)} %get-tuple-element.186, s32[]{:T(128)S(6)} %select_n.34), kind=kLoop, calls=%fused_computation.4.clone.1 | loop fusion | bytes 4194308 | tf_op jit(solution)/shard_map/while/body/dynamic_slice | solution.py:61
  27.9 1.2 fusion.42
  29.1 0.1 multiply_dynamic-update-slice_fusion.2
  29.2 3.3 %constant_dynamic-slice_fusion.4 = bf16[32,128,2,128]{3,2,1,0:T(2,128)(2,1)S(1)} fusion(bf16[32,384,2,128]{3,2,1,0:T(2,128)(2,1)} %get-tuple-element.186, s32[]{:T(128)S(6)} %select_n.34), kind=kLoop, calls=%fused_computation.4.clone.1 | loop fusion | bytes 4194308 | tf_op jit(solution)/shard_map/while/body/dynamic_slice | solution.py:61
  32.5 1.2 fusion.42
  33.6 0.1 multiply_dynamic-update-slice_fusion.2
  33.7 3.3 %constant_dynamic-slice_fusion.4 = bf16[32,128,2,128]{3,2,1,0:T(2,128)(2,1)S(1)} fusion(bf16[32,384,2,128]{3,2,1,0:T(2,128)(2,1)} %get-tuple-element.186, s32[]{:T(128)S(6)} %select_n.34), kind=kLoop, calls=%fused_computation.4.clone.1 | loop fusion | bytes 4194308 | tf_op jit(solution)/shard_map/while/body/dynamic_slice | solution.py:61
  37.0 1.2 fusion.42
  38.2 0.1 multiply_dynamic-update-slice_fusion.2
  38.2 0.1 fusion.19
  38.4 0.2 fusion.24
  38.6 0.2 divide_convert_fusion
  38.9 12.1 %while.21 = (s32[]{:T(128)}, f32[32,2,128]{2,1,0:T(2,128)S(1)}, s32[]{:T(128)}, bf16[32,2,384]{2,1,0:T(2,128)(2,1)S(1)}, bf16[32,384,2,128]{3,2,1,0:T(2,128)(2,1...) while((s32[]{:T(128)}, f32[32,2,128]{2,1,0:T(2,128)S(1)}, s32[]{:T(128)}, ...), condition=%wide.region_7.8_spmd, body=%wide.region_6.7_spmd.sunk | while | flops 2105350 | bytes 6471835 | solution.py:89
  38.9 3.3 %constant_dynamic-slice_fusion.5 = bf16[32,128,2,128]{3,2,1,0:T(2,128)(2,1)S(1)} fusion(bf16[32,384,2,128]{3,2,1,0:T(2,128)(2,1)} %get-tuple-element.214, s32[]{:T(128)S(6)} %select_n.35), kind=kLoop, calls=%fused_computation.9.clone.1 | loop fusion | bytes 4194308 | tf_op jit(solution)/shard_map/while/body/dynamic_slice | solution.py:84
  42.2 0.6 fusion.45
  42.9 3.3 %constant_dynamic-slice_fusion.5 = bf16[32,128,2,128]{3,2,1,0:T(2,128)(2,1)S(1)} fusion(bf16[32,384,2,128]{3,2,1,0:T(2,128)(2,1)} %get-tuple-element.214, s32[]{:T(128)S(6)} %select_n.35), kind=kLoop, calls=%fused_computation.9.clone.1 | loop fusion | bytes 4194308 | tf_op jit(solution)/shard_map/while/body/dynamic_slice | solution.py:84
  46.2 0.6 fusion.45
  46.9 3.3 %constant_dynamic-slice_fusion.5 = bf16[32,128,2,128]{3,2,1,0:T(2,128)(2,1)S(1)} fusion(bf16[32,384,2,128]{3,2,1,0:T(2,128)(2,1)} %get-tuple-element.214, s32[]{:T(128)S(6)} %select_n.35), kind=kLoop, calls=%fused_computation.9.clone.1 | loop fusion | bytes 4194308 | tf_op jit(solution)/shard_map/while/body/dynamic_slice | solution.py:84
  50.2 0.6 fusion.45
  51.0 0.1 add_convert_fusion.1
  51.1 2.2 convolution_convert_fusion.1
  53.3 25.0 %all-gather.8.cloned.1.call-done = bf16[256,2048]{1,0:T(8,128)(2,1)} async-done(((bf16[32,2048]{1,0:T(8,128)(2,1)}), bf16[256,2048]{1,0:T(8,128)(2,1)}) %all-gather.8.cloned.1.call-update) | async-done | bytes 1048592 | tf_op jit(solution)/shard_map/all_gather | solution.py:13
  78.3 1.4 reduce_sum.50
  79.7 0.9 convert_add_fusion
  80.6 0.7 multiply_convert_fusion
  81.4 5.3 %copy.57 = bf16[256,8,8,128]{3,1,2,0:T(8,128)(2,1)} copy(bf16[256,8,8,128]{3,2,1,0:T(8,128)(2,1)} %bitcast.71) | data formatting | bytes 8388608
  86.7 6.5 %copy.27 = bf16[1024,2048]{1,0:T(8,128)(2,1)} copy(bf16[1024,2048]{0,1:T(8,128)(2,1)} %bitcast.70) | data formatting | bytes 8388608 | tf_op jit(solution)/shard_map/dot_general | solution.py:111
  93.2 23.5 %all-gather.2 = bf16[16,32,8]{1,2,0:T(8,128)(2,1)S(1)} all-gather(bf16[1,32,8]{1,2,0:T(8,128)(2,1)S(1)} %convert_bitcast_fusion), channel_id=1, replica_groups=mesh['req'=16,'head'=8] {'req'}, dimensions={0}, use_global_device_ids=true | all-gather | bytes 8704 | tf_op jit(solution)/shard_map/all_gather | solution.py:18
  116.7 0.1 reshape.225
  116.8 23.1 %all-gather.1 = s32[16,32,8]{1,2,0:T(8,128)S(1)} all-gather(s32[1,32,8]{1,2,0:T(8,128)S(1)} %bitcast.79), channel_id=1, replica_groups=mesh['req'=16,'head'=8] {'req'}, dimensions={0}, use_global_device_ids=true | all-gather | bytes 17408 | tf_op jit(solution)/shard_map/all_gather | solution.py:18
  139.9 0.1 reshape.222
  140.1 0.1 select_reduce_fusion
  140.2 5.2 %fusion.8 = f32[512,8,1,2,64]{0,4,3,1,2:T(8,128)S(1)} fusion(bf16[8,2,64,2048]{3,2,1,0:T(8,128)(2,1)} %bitcast.72, bf16[512,2048]{1,0:T(8,128)(2,1)} %all-gather.6.cloned.1.call-done), kind=kOutput, calls=%fused_computation.15 | convolution fusion | flops 2147483648 | bytes 8388608 | tf_op jit(solution)/shard_map/dot_general | solution.py:111
  145.4 0.3 fusion.13
  145.7 1.2 copy-done.3
  147.0 2.6 %convolution_convert_fusion = bf16[512,2048]{1,0:T(8,128)(2,1)} fusion(bf16[512,512]{0,1:T(8,128)(2,1)S(1)} %bitcast.76, bf16[512,2048]{1,0:T(8,128)(2,1)S(1)} %bitcast.80), kind=kOutput, calls=%fused_computation.11 | convolution fusion | flops 1074790400 | bytes 4718592 | tf_op jit(solution)/shard_map/dot_general | solution.py:127
  149.7 71.5 %reduce-scatter.3.cloned.1.call-done = bf16[32,2048]{1,0:T(8,128)(2,1)} async-done(((bf16[512,2048]{1,0:T(8,128)(2,1)}), bf16[32,2048]{1,0:T(8,128)(2,1)}) %reduce-scatter.3.cloned.1.call-update) | async-done | bytes 131088 | tf_op jit(solution)/shard_map/reduce_scatter | solution.py:126
  221.2 31.8 %reduce-scatter.5.cloned.1.call-done = bf16[32,256]{1,0:T(8,128)(2,1)} async-done(((bf16[32,2048]{1,0:T(8,128)(2,1)}), bf16[32,256]{1,0:T(8,128)(2,1)}) %reduce-scatter.5.cloned.1.call-update) | async-done | bytes 16400 | tf_op jit(solution)/shard_map/reduce_scatter | solution.py:132
  253.0 1.4 add_convert_fusion
  (38 shorter events, 0.6 us)
Async XLA Ops:
  6.5 16.7 %copy-start = (bf16[3,2048,256]{2,1,0:T(8,128)(2,1)S(1)}, bf16[3,2048,256]{2,1,0:T(8,128)(2,1)}, u32[]{:S(2)}) copy-start(bf16[3,2048,256]{2,1,0:T(8,128)(2,1)} %param.18) | copy-start | bytes 9437188
  6.5 71.8 %all-gather.8.cloned.1.call-start = ((), (), s32[]{:S(2)}) async-start(), calls=%async_computation.5 | async-start | bytes 1179648 | tf_op jit(solution)/shard_map/all_gather | solution.py:13
  53.3 86.9 %all-gather.6.cloned.1.call-start = ((), (), s32[]{:S(2)}) async-start(), calls=%async_computation.2 | async-start | bytes 2228224 | tf_op jit(solution)/shard_map/all_gather | solution.py:18
  81.4 139.8 %reduce-scatter.3.cloned.1.call-start = ((), (), s32[]{:S(2)}) async-start(), calls=%async_computation.3 | async-start | bytes 2228224 | tf_op jit(solution)/shard_map/reduce_scatter | solution.py:126
  86.7 6.5 %copy-start.2 = (f32[32,8]{0,1:T(8,128)S(1)}, f32[32,8]{0,1:T(8,128)}, u32[]{:S(2)}) copy-start(f32[32,8]{0,1:T(8,128)} %param.17) | copy-start | bytes 3076
  86.7 30.1 %copy-start.1 = (s32[32,8]{0,1:T(8,128)S(1)}, s32[32,8]{0,1:T(8,128)}, u32[]{:S(2)}) copy-start(s32[32,8]{0,1:T(8,128)} %param.16) | copy-start | bytes 3076
  145.4 1.6 copy-start.3
  149.6 103.4 %reduce-scatter.5.cloned.1.call-start = ((), (), s32[]{:S(2)}) async-start(), calls=%async_computation.4 | async-start | bytes 147456 | tf_op jit(solution)/shard_map/reduce_scatter | solution.py:132
Sparse Core Ops, SparseCore 0:
  53.4 24.8 all-gather.7
  81.5 45.1 all-gather.5
  149.7 71.3 reduce-scatter.2
  223.5 29.4 reduce-scatter.4
